TPU v7x, 128 devices: a whole 4x4x4 slice. The times are simulated.
128 devices in a mesh: fsdp: 8 (over x, core), tensor: 2 (over y_lo), context: 8 (over z, y_hi).
Axes of the slice: x: 4, y: 4 (y_hi: 2, y_lo: 2; y = y_hi * 2 + y_lo), z: 4, core: 2. Of those that a mesh axis runs over, the one named last changes fastest.
Arguments:
- block_input: bfloat16 [16384, 768], P(('fsdp', 'context')), may hold values from -6 to 6
- seq_lengths: int32 [8, 3], P('fsdp'), may hold values from 1 to 1536, 2048 in all within a row
- attn_gain: bfloat16 [768], P('fsdp'), may hold values from 0.5 to 1.5
- qkv_weight: bfloat16 [768, 3, 768], P('fsdp', None, 'tensor'), may hold values from -0.3969283 to 0.3969283
- proj_weight: bfloat16 [768, 768], P('tensor', 'fsdp'), may hold values from -4 to 4
- mlp_gain: bfloat16 [768], P('fsdp'), may hold values from 0.5 to 1.5
- gelu_weight: bfloat16 [768, 2, 1152], P('fsdp', None, 'tensor'), may hold values from -0.21875 to 0.21875
- down_weight: bfloat16 [1152, 768], P('tensor', 'fsdp'), may hold values from -0.1875 to 0.1875
- out_cotangent: bfloat16 [16384, 768], P(('fsdp', 'context')), may hold values from -6 to 6
Outputs:
- block_output: bfloat16 [16384, 768], P(('fsdp', 'context'))
- input_grad: float32 [16384, 768], P(('fsdp', 'context'))
- attngain_grad: float32 [768], P('fsdp')
- qkv_grad: float32 [768, 3, 768], P('fsdp', None, 'tensor')
- proj_grad: float32 [768, 768], P('tensor', 'fsdp')
- mlpgain_grad: float32 [768], P('fsdp')
- gelu_grad: float32 [768, 2, 1152], P('fsdp', None, 'tensor')
- down_grad: float32 [1152, 768], P('tensor', 'fsdp')
All inputs are finite; a program needn't handle non-finite values.
Results may differ from a plain program's by a relative error of at most 0.02.
Values may be sent and summed in bfloat16 or wider, within the bound.
A program may use at most 128 MiB of HBM per device.

v0:
```python
import jax
import jax.numpy as jnp
from jax import lax
from jax.sharding import PartitionSpec as P

HD = 64
EPSILON = 1e-05
THETA = 160000.0
MASKED_LOW = -1e30


def layer_norm(values):
    centre = values - jnp.mean(values, axis=-1, keepdims=True)
    spread = lax.rsqrt(jnp.mean(centre * centre, axis=-1, keepdims=True) + EPSILON)
    return (centre * spread, spread)


def norm_back(grad_out, normed, spread, gain):
    scaled = grad_out * gain
    inner = jnp.mean(scaled, axis=-1, keepdims=True) + normed * jnp.mean(
        scaled * normed, axis=-1, keepdims=True
    )
    return spread * (scaled - inner)


def segments_of(row_ids, lengths):
    ends = jnp.cumsum(lengths)
    segment = jnp.sum((row_ids[:, None] >= ends[None, :]).astype(jnp.int32), axis=1)
    starts = ends - lengths
    picked = segment[:, None] == jnp.arange(lengths.shape[0], dtype=jnp.int32)[None, :]
    begin = jnp.sum(jnp.where(picked, starts[None, :], 0), axis=1)
    return (segment, row_ids - begin)


def rope_tables(positions, head_dim):
    half_dim = head_dim // 2
    exponent = jnp.arange(half_dim, dtype=jnp.float32) * (-2.0 / head_dim)
    frequency = jnp.power(jnp.float32(THETA), exponent)
    angles = positions.astype(jnp.float32)[:, None] * frequency[None, :]
    return (jnp.cos(angles)[:, None, :], jnp.sin(angles)[:, None, :])


def rotate(values, cosine, sine_tab):
    half_dim = values.shape[-1] // 2
    lower_half, upper_half = (values[..., :half_dim], values[..., half_dim:])
    return jnp.concatenate(
        [lower_half * cosine - upper_half * sine_tab, upper_half * cosine + lower_half * sine_tab],
        axis=-1,
    )


def rotate_back(grads, cosine, sine_tab):
    half_dim = grads.shape[-1] // 2
    lower_half, upper_half = (grads[..., :half_dim], grads[..., half_dim:])
    return jnp.concatenate(
        [lower_half * cosine + upper_half * sine_tab, upper_half * cosine - lower_half * sine_tab],
        axis=-1,
    )


def gelu_parts(gate_pre):
    normal_cdf = 0.5 * (1.0 + jax.scipy.special.erf(gate_pre * 0.7071067811865476))
    density = jnp.exp(-0.5 * gate_pre * gate_pre) * 0.3989422804014327
    return (gate_pre * normal_cdf, normal_cdf + gate_pre * density)


def split_count(row_count):
    pieces = 1
    while row_count // pieces > 1024 and row_count % (2 * pieces) == 0:
        pieces = pieces * 2
    return pieces


def over_blocks(step, running, members):
    row_count = members[0].shape[0]
    pieces = split_count(row_count)
    stride = row_count // pieces

    def one_block(counter, current):
        offset = counter * stride
        sliced = tuple((lax.dynamic_slice_in_dim(member, offset, stride, 0) for member in members))
        return step(current, sliced, offset)

    return lax.fori_loop(0, pieces, one_block, running)


def guarded(step):

    def wrapped(running, members, first_row):
        return step(running, members, first_row)

    def folded(running, members, first_row):
        return over_blocks(wrapped, running, members)

    return folded


def on_device(
    block_input,
    seq_lengths,
    attn_gain,
    qkv_weight,
    proj_weight,
    mlp_gain,
    gelu_weight,
    down_weight,
    out_cotangent,
):
    row_count = block_input.shape[0]
    feature_count = block_input.shape[1]
    lengths = seq_lengths[0]
    group_rows = row_count * lax.axis_size("context")
    own_first = lax.axis_index("context") * row_count
    own_rows = own_first + jnp.arange(row_count, dtype=jnp.int32)
    own_segment, positions = segments_of(own_rows, lengths)
    cosine, sine_tab = rope_tables(positions, HD)
    gathered = (
        lax.all_gather(qkv_weight, "fsdp", axis=0, tiled=True),
        lax.all_gather(proj_weight, "fsdp", axis=1, tiled=True),
        lax.all_gather(gelu_weight, "fsdp", axis=0, tiled=True),
        lax.all_gather(down_weight, "fsdp", axis=1, tiled=True),
        lax.all_gather(attn_gain, "fsdp", axis=0, tiled=True),
        lax.all_gather(mlp_gain, "fsdp", axis=0, tiled=True),
    )
    qkv_full, proj_full, gelu_full, down_full, attn_full, mlp_full = gathered
    local_width = qkv_full.shape[2]
    head_count = local_width // HD
    hidden = gelu_full.shape[2]
    attn_scale = attn_full.astype(jnp.float32)
    mlp_scale = mlp_full.astype(jnp.float32)
    inputs = block_input.astype(jnp.float32)
    normed_attn, spread_attn = layer_norm(inputs)
    hidden_attn = (normed_attn * attn_scale).astype(jnp.bfloat16)
    qkv_flat = qkv_full.reshape(feature_count, 3 * local_width)
    projected = jnp.dot(hidden_attn, qkv_flat, preferred_element_type=jnp.float32).reshape(
        row_count, 3, head_count, HD
    )
    query_bf = rotate(projected[:, 0], cosine, sine_tab).astype(jnp.bfloat16)
    key_bf = rotate(projected[:, 1], cosine, sine_tab).astype(jnp.bfloat16)
    value_bf = projected[:, 2].astype(jnp.bfloat16)
    key_flat = key_bf.reshape(row_count, local_width)
    value_flat = value_bf.reshape(row_count, local_width)
    keys_group, values_group = (
        lax.all_gather(key_flat, "context", axis=0, tiled=True),
        lax.all_gather(value_flat, "context", axis=0, tiled=True),
    )
    keys_heads = keys_group.reshape(group_rows, head_count, HD)
    values_heads = values_group.reshape(group_rows, head_count, HD)
    group_segment, unused_pos = segments_of(jnp.arange(group_rows, dtype=jnp.int32), lengths)
    same_group = (own_segment[:, None] == group_segment[None, :])[None]
    fwd_scores = (
        jnp.einsum("qhd,khd->hqk", query_bf, keys_heads, preferred_element_type=jnp.float32) * 0.125
    )
    row_max = jnp.max(jnp.where(same_group, fwd_scores, MASKED_LOW), axis=2)
    denom_sum = jnp.sum(
        jnp.where(same_group, jnp.exp(fwd_scores - row_max[:, :, None]), 0.0), axis=2
    )
    log_total = row_max + jnp.log(denom_sum)
    fwd_weights = jnp.where(same_group, jnp.exp(fwd_scores - log_total[:, :, None]), 0.0).astype(
        jnp.bfloat16
    )
    mixed = jnp.einsum(
        "hqk,khd->qhd", fwd_weights, values_heads, preferred_element_type=jnp.float32
    ).astype(jnp.bfloat16)
    mixed_flat = mixed.reshape(row_count, local_width)
    attn_part = jnp.dot(mixed_flat, proj_full, preferred_element_type=jnp.float32)
    residual = inputs + lax.psum(attn_part, "tensor")
    normed_mlp, spread_mlp = layer_norm(residual)
    hidden_mlp = (normed_mlp * mlp_scale).astype(jnp.bfloat16)
    gelu_flat = gelu_full.reshape(feature_count, 2 * hidden)
    gate_up = jnp.dot(hidden_mlp, gelu_flat, preferred_element_type=jnp.float32).reshape(
        row_count, 2, hidden
    )
    gate_pre, up_pre = (gate_up[:, 0], gate_up[:, 1])
    gelu_val, gelu_slope = gelu_parts(gate_pre)
    activ = (gelu_val * up_pre).astype(jnp.bfloat16)
    mlp_part = jnp.dot(activ, down_full, preferred_element_type=jnp.float32)
    block_output = (
        residual + lax.psum(mlp_part.astype(jnp.bfloat16), "tensor").astype(jnp.float32)
    ).astype(jnp.bfloat16)
    act_grad = jnp.dot(out_cotangent, down_full.T, preferred_element_type=jnp.float32)
    down_grad_t = jnp.dot(out_cotangent.T, activ, preferred_element_type=jnp.float32)
    gate_up_grad = (
        jnp.stack([act_grad * up_pre * gelu_slope, act_grad * gelu_val], axis=1)
        .astype(jnp.bfloat16)
        .reshape(row_count, 2 * hidden)
    )
    gelu_grad = jnp.dot(hidden_mlp.T, gate_up_grad, preferred_element_type=jnp.float32).reshape(
        feature_count, 2, hidden
    )
    mlp_in_grad = lax.psum(
        jnp.dot(gate_up_grad, gelu_flat.T, preferred_element_type=jnp.float32), "tensor"
    )
    mlpgain_grad = jnp.sum(mlp_in_grad * normed_mlp, axis=0)
    resid_grad = out_cotangent.astype(jnp.float32) + norm_back(
        mlp_in_grad, normed_mlp, spread_mlp, mlp_scale
    )
    resid_bf = resid_grad.astype(jnp.bfloat16)
    out_grad = jnp.dot(resid_bf, proj_full.T, preferred_element_type=jnp.float32).astype(
        jnp.bfloat16
    )
    proj_grad_t = jnp.dot(resid_bf.T, mixed_flat, preferred_element_type=jnp.float32)
    out_heads = out_grad.reshape(row_count, head_count, HD)
    delta = jnp.transpose(
        jnp.sum(out_heads.astype(jnp.float32) * mixed.astype(jnp.float32), axis=2)
    )

    def key_terms(members, first_row):
        key_count = members[0].shape[0]
        key_part = members[0].reshape(key_count, head_count, HD)
        value_part = members[1].reshape(key_count, head_count, HD)
        key_segment, unused = segments_of(
            first_row + jnp.arange(key_count, dtype=jnp.int32), lengths
        )
        same_doc = (own_segment[:, None] == key_segment[None, :])[None]
        scores = (
            jnp.einsum("qhd,khd->hqk", query_bf, key_part, preferred_element_type=jnp.float32)
            * 0.125
        )
        weights = jnp.where(same_doc, jnp.exp(scores - log_total[:, :, None]), 0.0)
        prob_grad = jnp.einsum(
            "qhd,khd->hqk", out_heads, value_part, preferred_element_type=jnp.float32
        )
        score_grad = (weights * (prob_grad - delta[:, :, None])).astype(jnp.bfloat16)
        return (key_part, weights, score_grad)

    def owner_step(running, members, first_row):
        query_grad, key_all, value_all = running
        key_part, weights, score_grad = key_terms(members, first_row)
        key_count = key_part.shape[0]
        query_grad = (
            query_grad
            + jnp.einsum("hqk,khd->qhd", score_grad, key_part, preferred_element_type=jnp.float32)
            * 0.125
        )
        key_piece = (
            jnp.einsum(
                "hqk,qhd->khd", score_grad, query_bf, preferred_element_type=jnp.float32
            ).reshape(key_count, local_width)
            * 0.125
        )
        value_piece = jnp.einsum(
            "hqk,qhd->khd",
            weights.astype(jnp.bfloat16),
            out_heads,
            preferred_element_type=jnp.float32,
        ).reshape(key_count, local_width)
        key_all = lax.dynamic_update_slice_in_dim(
            key_all,
            lax.dynamic_slice_in_dim(key_all, first_row, key_count, 0) + key_piece,
            first_row,
            0,
        )
        value_all = lax.dynamic_update_slice_in_dim(
            value_all,
            lax.dynamic_slice_in_dim(value_all, first_row, key_count, 0) + value_piece,
            first_row,
            0,
        )
        return (query_grad, key_all, value_all)

    grad_start = jnp.zeros((row_count, head_count, HD), jnp.float32)
    back_state = (
        grad_start,
        jnp.zeros((group_rows, local_width), jnp.float32),
        jnp.zeros((group_rows, local_width), jnp.float32),
    )
    back_result = guarded(owner_step)(
        back_state,
        (
            lax.all_gather(key_flat, "context", axis=0, tiled=True),
            lax.all_gather(value_flat, "context", axis=0, tiled=True),
        ),
        jnp.int32(0),
    )
    query_grad = back_result[0]
    key_grad, value_grad = (
        lax.psum_scatter(
            back_result[1].astype(jnp.bfloat16), "context", scatter_dimension=0, tiled=True
        ).astype(jnp.float32),
        lax.psum_scatter(
            back_result[2].astype(jnp.bfloat16), "context", scatter_dimension=0, tiled=True
        ).astype(jnp.float32),
    )
    key_grad = key_grad.reshape(row_count, head_count, HD)
    value_grad = value_grad.reshape(row_count, head_count, HD)
    qkv_rows = (
        jnp.stack(
            [
                rotate_back(query_grad, cosine, sine_tab),
                rotate_back(key_grad, cosine, sine_tab),
                value_grad,
            ],
            axis=1,
        )
        .astype(jnp.bfloat16)
        .reshape(row_count, 3 * local_width)
    )
    qkv_grad = jnp.dot(hidden_attn.T, qkv_rows, preferred_element_type=jnp.float32).reshape(
        feature_count, 3, local_width
    )
    attn_in_grad = lax.psum(
        jnp.dot(qkv_rows, qkv_flat.T, preferred_element_type=jnp.float32).astype(jnp.bfloat16),
        "tensor",
    ).astype(jnp.float32)
    attngain_grad = jnp.sum(attn_in_grad * normed_attn, axis=0)
    input_grad = resid_grad + norm_back(attn_in_grad, normed_attn, spread_attn, attn_scale)
    grads = (
        attngain_grad[:, None],
        mlpgain_grad[:, None],
        qkv_grad.reshape(feature_count, 3 * local_width),
        gelu_grad.reshape(feature_count, 2 * hidden),
        proj_grad_t,
        down_grad_t,
    )
    widths = [g.shape[1] for g in grads]
    packed = jnp.concatenate(grads, axis=1)
    packed = lax.psum_scatter(packed, "fsdp", scatter_dimension=0, tiled=True)
    packed = lax.psum(packed, "context")
    pieces = []
    start = 0
    for width in widths:
        pieces.append(packed[:, start : start + width])
        start += width
    shard_rows = packed.shape[0]
    shares = (
        pieces[0][:, 0],
        pieces[2].reshape(shard_rows, 3, local_width),
        pieces[4].T,
        pieces[1][:, 0],
        pieces[3].reshape(shard_rows, 2, hidden),
        pieces[5].T,
    )
    return (
        block_output,
        input_grad,
        shares[0],
        shares[1],
        shares[2],
        shares[3],
        shares[4],
        shares[5],
    )


def solution(mesh):
    in_specs = (
        P(("fsdp", "context"), None),
        P("fsdp", None),
        P("fsdp"),
        P("fsdp", None, "tensor"),
        P("tensor", "fsdp"),
        P("fsdp"),
        P("fsdp", None, "tensor"),
        P("tensor", "fsdp"),
        P(("fsdp", "context"), None),
    )
    out_specs = (
        P(("fsdp", "context"), None),
        P(("fsdp", "context"), None),
        P("fsdp"),
        P("fsdp", None, "tensor"),
        P("tensor", "fsdp"),
        P("fsdp"),
        P("fsdp", None, "tensor"),
        P("tensor", "fsdp"),
    )
    return jax.shard_map(
        on_device, mesh=mesh, in_specs=in_specs, out_specs=out_specs, check_vma=False
    )
```

profile of v0, /device:TPU:0, one launch (start us, length us, event | category | flops | bytes accessed | tf_op | source)
XLA Modules:
  0.0 698.4 jit_solution(5407401806397029626)
XLA Ops:
  11.6 14.7 %all-reduce.2 = (bf16[768]{0:T(1024)(128)(2,1)S(1)}, bf16[768]{0:T(1024)(128)(2,1)S(1)}) all-reduce(bf16[768]{0:T(1024)(128)(2,1)S(1)} %dynamic-update-slice, bf16[768]{0:T(1024)(128)(2,1)S(1)} %dynamic-update-slice.1), channel_id=1, replica_groups=mesh['fsdp'=8,'tensor'=2,'context'=8] {'fsdp'}, use_global_device_ids=true, to_apply=%add | all-reduce | flops 1536 | bytes 6144
  30.6 6.5 all-gather.5.cloned.1.call-done
  37.1 2.6 copy.52
  45.6 13.2 %all_gather.30 = bf16[384,768]{0,1:T(8,128)(2,1)S(1)} all-gather(bf16[384,96]{0,1:T(8,128)(2,1)S(1)} %copy-done.46), channel_id=1, replica_groups=mesh['fsdp'=8,'tensor'=2,'context'=8] {'fsdp'}, dimensions={1}, use_global_device_ids=true | all-gather | bytes 663552 | tf_op jit(solution)/shard_map/all_gather | solution.py:119
  58.8 33.9 %all-gather.9.cloned.1.call-done = bf16[2048,384]{0,1:T(8,128)(2,1)} async-done(((bf16[256,384]{0,1:T(8,128)(2,1)}), bf16[2048,384]{0,1:T(8,128)(2,1)}) %all-gather.9.cloned.1.call-update) | async-done | bytes 1572880 | tf_op jit(solution)/shard_map/all_gather | solution.py:144
  92.7 3.9 select_reduce_fusion.1
  96.6 3.9 select_reduce_fusion
  101.1 42.2 %all-gather.7.cloned.1.call-done = bf16[2048,384]{0,1:T(8,128)(2,1)} async-done(((bf16[256,384]{0,1:T(8,128)(2,1)}), bf16[2048,384]{0,1:T(8,128)(2,1)}) %all-gather.7.cloned.1.call-update) | async-done | bytes 1572880 | tf_op jit(solution)/shard_map/all_gather | solution.py:145
  143.3 7.7 %fusion.13 = bf16[6,64,256]{2,1,0:T(8,128)(2,1)S(1)} fusion(bf16[2048,6,64]{0,2,1:T(8,128)(2,1)} %bitcast.184, f32[6,256,2048]{2,1,0:T(8,128)} %copy-done.7, f32[6,256]{1,0:T(8,128)S(1)} %log_add_fusion, pred[256,2048]{1,0:T(8,128)(4,1)S(1)} %broadcast_compare_fusion.1), kind=kOutput, calls=%fused_computation.37 | convolution fusion | flops 415334400 | bytes 14882816 | tf_op jit(solution)/shard_map/hqk,khd->qhd/dot_general | solution.py:162
  152.4 16.8 %all_gather.33 = bf16[576,768]{0,1:T(8,128)(2,1)} all-gather(bf16[576,96]{0,1:T(8,128)(2,1)S(1)} %copy-done.45), channel_id=1, replica_groups=mesh['fsdp'=8,'tensor'=2,'context'=8] {'fsdp'}, dimensions={1}, use_global_device_ids=true | all-gather | bytes 995328 | tf_op jit(solution)/shard_map/all_gather | solution.py:121
  170.0 2.7 copy.54
  172.7 40.8 %all-reduce.9.cloned.1.call-done = f32[256,768]{1,0:T(8,128)} async-done(((f32[256,768]{1,0:T(8,128)}), f32[256,768]{1,0:T(8,128)}) %all-reduce.9.cloned.1.call-update) | async-done | bytes 786448 | tf_op jit(solution)/shard_map/psum | solution.py:167
  219.8 41.8 %all-reduce.11.cloned.1.call-done = f32[256,768]{1,0:T(8,128)} async-done(((f32[256,768]{1,0:T(8,128)}), f32[256,768]{1,0:T(8,128)}) %all-reduce.11.cloned.1.call-update) | async-done | bytes 786448 | tf_op jit(solution)/shard_map/psum | solution.py:191
  261.6 2.1 multiply_reduce_fusion
  266.4 2.1 broadcast.210
  270.5 40.4 %while.20 = (s32[]{:T(128)}, f32[256,6,64]{0,2,1:T(8,128)}, f32[2048,384]{0,1:T(8,128)}, f32[2048,384]{0,1:T(8,128)}, bf16[2048,384]{0,1:T(8,128)(2,1)}, /*index...) while((s32[]{:T(128)}, f32[256,6,64]{0,2,1:T(8,128)}, ...), condition=%wide.region_19.20_spmd.clone, body=%wide.region_17.19_spmd.clone.sunk | while | flops 1024107520 | bytes 131182336 | solution.py:84
  275.0 3.3 fusion.105
  278.4 2.6 fusion.106
  281.0 4.3 fusion.107
  295.2 3.3 fusion.105
  298.6 2.7 fusion.106
  301.2 4.3 fusion.107
  310.9 3.4 convert_element_type.160
  318.9 2.7 fusion.48
  321.6 67.5 %reduce-scatter.4.cloned.1.call-done = bf16[256,384]{0,1:T(8,128)(2,1)} async-done(((bf16[2048,384]{0,1:T(8,128)(2,1)}), bf16[256,384]{0,1:T(8,128)(2,1)}) %reduce-scatter.4.cloned.1.call-update) | async-done | bytes 196624 | tf_op jit(solution)/shard_map/reduce_scatter | solution.py:278
  391.1 74.7 %reduce-scatter.6.cloned.1.call-done = bf16[256,384]{0,1:T(8,128)(2,1)} async-done(((bf16[2048,384]{0,1:T(8,128)(2,1)}), bf16[256,384]{0,1:T(8,128)(2,1)}) %reduce-scatter.6.cloned.1.call-update) | async-done | bytes 196624 | tf_op jit(solution)/shard_map/reduce_scatter | solution.py:281
  469.1 3.0 convolution_bitcast_fusion
  473.7 2.6 fusion.45
  476.3 32.8 %all-reduce.15.cloned.1.call-done = (bf16[256,768]{1,0:T(8,128)(2,1)}, bf16[256,768]{1,0:T(8,128)(2,1)}) async-done(((bf16[256,768]{1,0:T(8,128)(2,1)}, bf16[256,768]{1,0:T(8,128)(2,1)}), (bf16[256,768]{1,0:T(8,128)(2,1)}, bf16[256,768]{1,0:T(8,128)(2,1)})) %all-reduce.15.cloned.1.call-update) | async-done | bytes 786448 | tf_op jit(solution)/shard_map/psum | solution.py:179
  510.7 13.5 %concatenate.21 = f32[768,3266]{1,0:T(8,128)} concatenate(f32[768,1]{1,0:T(8,128)S(1)} %broadcast_in_dim.141, f32[768,1]{1,0:T(8,128)S(1)} %broadcast_in_dim.142, f32[768,1152]{1,0:T(8,128)} %fusion.45, f32[768,1152]{1,0:T(8,128)} %fusion.48, f32[768,384]{1,0:T(8,128)} %fusion.38, f32[768,576]{1,0:T(8,128)} %convolution_bitcast_fusion), dimensions={1} | concatenate | bytes 20066304 | tf_op jit(solution)/shard_map/concatenate | solution.py:317
  524.3 62.2 %reduce-scatter.8.cloned.1.call-done = f32[96,3266]{1,0:T(8,128)} async-done(((f32[768,3266]{1,0:T(8,128)}), f32[96,3266]{1,0:T(8,128)}) %reduce-scatter.8.cloned.1.call-update) | async-done | bytes 1254160 | tf_op jit(solution)/shard_map/reduce_scatter | solution.py:318
  588.6 94.9 %all-reduce.13.cloned.1.call-done = f32[96,3266]{1,0:T(8,128)} async-done(((f32[96,3266]{1,0:T(8,128)}), f32[96,3266]{1,0:T(8,128)}) %all-reduce.13.cloned.1.call-update) | async-done | bytes 1254160 | tf_op jit(solution)/shard_map/psum | solution.py:319
  (264 shorter events, 70.3 us)
Async XLA Ops:
  7.2 32.6 %copy-start.10 = (bf16[256,768]{1,0:T(8,128)(2,1)S(1)}, bf16[256,768]{1,0:T(8,128)(2,1)}, u32[]{:S(2)}) copy-start(bf16[256,768]{1,0:T(8,128)(2,1)} %param.11) | copy-start | bytes 1179652
  7.2 29.9 %all-gather.5.cloned.1.call-start = ((), (), s32[]{:S(2)}) async-start(), calls=%async_computation.3 | async-start | bytes 1990656 | tf_op jit(solution)/shard_map/all_gather | solution.py:118
  7.9 84.8 %all-gather.9.cloned.1.call-start = ((), (), s32[]{:S(2)}) async-start(), calls=%async_computation.5 | async-start | bytes 1769472 | tf_op jit(solution)/shard_map/all_gather | solution.py:144
  30.3 10.2 %copy-start.50 = (f32[256]{0:T(256)}, f32[256]{0:T(256)S(1)}, u32[]{:S(2)}) copy-start(f32[256]{0:T(256)S(1)} %add_rsqrt_fusion.1) | copy-start | bytes 3076
  30.6 11.1 %copy-start.40 = (f32[256,32]{0,1:T(8,128)}, f32[256,32]{0,1:T(8,128)S(1)}, u32[]{:S(2)}) copy-start(f32[256,32]{0,1:T(8,128)S(1)} %get-tuple-element.417) | copy-start | bytes 98308
  30.6 11.1 %copy-start.41 = (f32[256,32]{0,1:T(8,128)}, f32[256,32]{0,1:T(8,128)S(1)}, u32[]{:S(2)}) copy-start(f32[256,32]{0,1:T(8,128)S(1)} %get-tuple-element.418) | copy-start | bytes 98308
  41.8 54.8 %copy-start.33 = (bf16[256,6,32]{0,2,1:T(8,128)(2,1)}, bf16[256,6,32]{0,2,1:T(8,128)(2,1)S(1)}, u32[]{:S(2)}) copy-start(bf16[256,6,32]{0,2,1:T(8,128)(2,1)S(1)} %get-tuple-element.409) | copy-start | bytes 294916
  41.8 54.8 %copy-start.35 = (bf16[256,6,32]{0,2,1:T(8,128)(2,1)}, bf16[256,6,32]{0,2,1:T(8,128)(2,1)S(1)}, u32[]{:S(2)}) copy-start(bf16[256,6,32]{0,2,1:T(8,128)(2,1)S(1)} %get-tuple-element.410) | copy-start | bytes 294916
  42.5 100.8 %all-gather.7.cloned.1.call-start = ((), (), s32[]{:S(2)}) async-start(), calls=%async_computation.4 | async-start | bytes 1769472 | tf_op jit(solution)/shard_map/all_gather | solution.py:145
  44.3 125.7 %all-gather.11.cloned.1.call-start = ((), (), s32[]{:S(2)}) async-start(), calls=%async_computation.7 | async-start | bytes 2211840 | tf_op jit(solution)/shard_map/all_gather | solution.py:120
  45.1 168.4 %all-reduce.9.cloned.1.call-start = ((), (), s32[]{:S(2)}) async-start(), calls=%async_computation.6 | async-start | bytes 1572864 | tf_op jit(solution)/shard_map/psum | solution.py:167
  58.8 92.1 %copy-start.19 = (bf16[384,768]{0,1:T(8,128)(2,1)}, bf16[384,768]{0,1:T(8,128)(2,1)S(1)}, u32[]{:S(2)}) copy-start(bf16[384,768]{0,1:T(8,128)(2,1)S(1)} %all_gather.30) | copy-start | bytes 1769476
  101.1 49.8 %copy-start.58 = (f32[6,256]{1,0:T(8,128)}, f32[6,256]{1,0:T(8,128)S(1)}, u32[]{:S(2)}) copy-start(f32[6,256]{1,0:T(8,128)S(1)} %log_add_fusion) | copy-start | bytes 18436
  143.3 9.1 %copy-start.45 = (bf16[576,96]{0,1:T(8,128)(2,1)S(1)}, bf16[576,96]{0,1:T(8,128)(2,1)}, u32[]{:S(2)}) copy-start(bf16[576,96]{0,1:T(8,128)(2,1)} %param.18) | copy-start | bytes 331780
  152.3 109.3 %all-reduce.11.cloned.1.call-start = ((), (), s32[]{:S(2)}) async-start(), calls=%async_computation.8 | async-start | bytes 1572864 | tf_op jit(solution)/shard_map/psum | solution.py:191
  172.7 44.1 %copy-start.31 = (bf16[256,768]{1,0:T(8,128)(2,1)S(1)}, bf16[256,768]{1,0:T(8,128)(2,1)}, u32[]{:S(2)}) copy-start(bf16[256,768]{1,0:T(8,128)(2,1)} %param.19) | copy-start | bytes 1179652
  214.9 48.9 %copy-start.8 = (f32[256,768]{1,0:T(8,128)}, f32[256,768]{1,0:T(8,128)S(1)}, u32[]{:S(2)}) copy-start(f32[256,768]{1,0:T(8,128)S(1)} %get-tuple-element.396) | copy-start | bytes 2359300
  217.5 46.2 %copy-start.42 = (bf16[256,1,576]{0,2,1:T(8,128)(2,1)}, bf16[256,1,576]{0,2,1:T(8,128)(2,1)S(1)}, u32[]{:S(2)}) copy-start(bf16[256,1,576]{0,2,1:T(8,128)(2,1)S(1)} %get-tuple-element.399) | copy-start | bytes 884740
  217.5 46.2 %copy-start.43 = (bf16[256,1,576]{0,2,1:T(8,128)(2,1)}, bf16[256,1,576]{0,2,1:T(8,128)(2,1)S(1)}, u32[]{:S(2)}) copy-start(bf16[256,1,576]{0,2,1:T(8,128)(2,1)S(1)} %get-tuple-element.400) | copy-start | bytes 884740
  217.5 44.1 %copy-start.48 = (f32[256]{0:T(256)S(1)}, f32[256]{0:T(256)}, u32[]{:S(2)}) copy-start(f32[256]{0:T(256)} %copy-done.47) | copy-start | bytes 3076
  217.5 44.1 %copy-start.53 = (f32[256]{0:T(256)S(1)}, f32[256]{0:T(256)}, u32[]{:S(2)}) copy-start(f32[256]{0:T(256)} %copy-done.52) | copy-start | bytes 3076
  217.8 45.9 %copy-start.32 = (bf16[256,768]{1,0:T(8,128)(2,1)S(1)}, bf16[256,768]{1,0:T(8,128)(2,1)}, u32[]{:S(2)}) copy-start(bf16[256,768]{1,0:T(8,128)(2,1)} %param.19) | copy-start | bytes 1179652
  219.6 45.6 %copy-start.20 = (bf16[384,768]{0,1:T(8,128)(2,1)S(1)}, bf16[384,768]{0,1:T(8,128)(2,1)}, u32[]{:S(2)}) copy-start(bf16[384,768]{0,1:T(8,128)(2,1)} %copy-done.19) | copy-start | bytes 1769476
  219.6 169.6 %reduce-scatter.4.cloned.1.call-start = ((), (), s32[]{:S(2)}) async-start(), calls=%async_computation.9 | async-start | bytes 1769472 | tf_op jit(solution)/shard_map/reduce_scatter | solution.py:278
  314.4 151.4 %reduce-scatter.6.cloned.1.call-start = ((), (), s32[]{:S(2)}) async-start(), calls=%async_computation.10 | async-start | bytes 1769472 | tf_op jit(solution)/shard_map/reduce_scatter | solution.py:281
  315.9 193.2 %all-reduce.15.cloned.1.call-start = ((), (), s32[]{:S(2)}) async-start(), calls=%async_computation.13 | async-start | bytes 1572864 | tf_op jit(solution)/shard_map/psum | solution.py:179
  318.9 71.2 %copy-start.14 = (f32[256,6,64]{0,2,1:T(8,128)S(1)}, f32[256,6,64]{0,2,1:T(8,128)}, u32[]{:S(2)}) copy-start(f32[256,6,64]{0,2,1:T(8,128)} %get-tuple-element.285) | copy-start | bytes 1179652
  318.9 148.7 %copy-start.13 = (bf16[768,3,384]{0,2,1:T(8,128)(2,1)S(1)}, bf16[768,3,384]{0,2,1:T(8,128)(2,1)}, u32[]{:S(2)}) copy-start(bf16[768,3,384]{0,2,1:T(8,128)(2,1)} %copy-done.12) | copy-start | bytes 5308420
  469.1 117.4 %reduce-scatter.8.cloned.1.call-start = ((), (), s32[]{:S(2)}) async-start(), calls=%async_computation.11 | async-start | bytes 11501568 | tf_op jit(solution)/shard_map/reduce_scatter | solution.py:318
  524.2 62.3 %copy-start.39 = (bf16[256,768]{1,0:T(8,128)(2,1)S(1)}, bf16[256,768]{1,0:T(8,128)(2,1)}, u32[]{:S(2)}) copy-start(bf16[256,768]{1,0:T(8,128)(2,1)} %get-tuple-element.393) | copy-start | bytes 1179652
  524.2 63.2 %copy-start.30 = (bf16[256,768]{1,0:T(8,128)(2,1)S(1)}, bf16[256,768]{1,0:T(8,128)(2,1)}, u32[]{:S(2)}) copy-start(bf16[256,768]{1,0:T(8,128)(2,1)} %get-tuple-element.394) | copy-start | bytes 1179652
  524.3 159.2 %all-reduce.13.cloned.1.call-start = ((), (), s32[]{:S(2)}) async-start(), calls=%async_computation.12 | async-start | bytes 2555904 | tf_op jit(solution)/shard_map/psum | solution.py:319
  (57 other events, 174.0 us)
Sparse Core Ops, SparseCore 0:
  9.7 27.3 all-gather.4
  42.7 50.0 all-gather.8
  95.5 47.7 all-gather.6
  145.4 24.5 all-gather.10
  172.8 40.5 all-reduce.8
  219.7 41.8 all-reduce.10
  314.5 74.6 reduce-scatter.3
  393.3 72.4 reduce-scatter.5
  469.2 39.8 all-reduce.14
  524.4 62.0 reduce-scatter.7
  589.2 94.2 all-reduce.12
where the time goes:
time: 700 us; the launch traced here: 698 us
  waiting for transfers between devices  499 us (71%)
  matrix products  54.2 us (8%)
  local copies, waits for them, and re-layouts  54.1 us (8%)
  blocking collectives  44.7 us (6%)
  other arithmetic  30.3 us (4%)
  between operations  15.2 us (2%)
    psum x1, waiting for transfers between devices, on_device(): packed = lax.psum(packed, 'context')  94.9 us
    reduce_scatter x1, waiting for transfers between devices, on_device(): lax.psum_scatter(back_result[2].astype(jnp.bfloat16), 'context', scatter_...  74.7 us
    reduce_scatter x1, waiting for transfers between devices, on_device(): lax.psum_scatter(back_result[1].astype(jnp.bfloat16), 'context', scatter_...  67.5 us
    reduce_scatter x1, waiting for transfers between devices, on_device(): packed = lax.psum_scatter(packed, 'fsdp', scatter_dimension=0, tiled=True)  62.2 us
    all_gather x1, waiting for transfers between devices, on_device(): lax.all_gather(value_flat, 'context', axis=0, tiled=True)  42.2 us
    psum x1, waiting for transfers between devices, on_device(): lax.psum(jnp.dot(gate_up_grad, gelu_flat.T, preferred_element_type=jnp.fl...  41.8 us
    psum x1, waiting for transfers between devices, on_device(): residual = inputs + lax.psum(attn_part, 'tensor')  40.8 us
    all_gather x1, waiting for transfers between devices, on_device(): lax.all_gather(key_flat, 'context', axis=0, tiled=True)  33.9 us
  transfers between devices with their start and end apart: 11, of which 11 were waited for; matrix products, arithmetic and copies ran while one was open for 7% of the time, Pallas kernels for 0%

commit v1 on v0

--- a/solution.py
+++ b/solution.py
@@ -2,6 +2,7 @@
 import jax.numpy as jnp
 from jax import lax
 from jax.sharding import PartitionSpec as P
+from jax.lax import all_gather
 
 HD = 64
 EPSILON = 1e-05
@@ -106,6 +107,11 @@
     down_weight,
     out_cotangent,
 ):
+
+    def _drive_task(field, peer_axis):
+        view_out = all_gather(field, axis_name=peer_axis).sum(axis=0)
+        return view_out
+
     row_count = block_input.shape[0]
     feature_count = block_input.shape[1]
     lengths = seq_lengths[0]
@@ -316,7 +322,7 @@
     widths = [g.shape[1] for g in grads]
     packed = jnp.concatenate(grads, axis=1)
     packed = lax.psum_scatter(packed, "fsdp", scatter_dimension=0, tiled=True)
-    packed = lax.psum(packed, "context")
+    packed = _drive_task(packed, "context")
     pieces = []
     start = 0
     for width in widths:

time: 700 us -> 730 us (1.043)
  waiting for transfers between devices: 499 us -> 528 us
    all_gather x0 -> x1, waiting for transfers between devices: none -> 124 us  [_drive_task(): view_out = all_gather(field, axis_name=peer_axis).sum(axis=0)]
    psum x1 -> x0, waiting for transfers between devices: 94.9 us -> none  [on_device(): packed = lax.psum(packed, 'context')]
where the time goes in v1:
time: 730 us; the launch traced here: 728 us
  waiting for transfers between devices  528 us (72%)
  matrix products  54.2 us (7%)
  local copies, waits for them, and re-layouts  50.2 us (7%)
  blocking collectives  44.7 us (6%)
  other arithmetic  34.8 us (5%)
  between operations  15.2 us (2%)
    all_gather x1, waiting for transfers between devices, _drive_task(): view_out = all_gather(field, axis_name=peer_axis).sum(axis=0)  124 us
    reduce_scatter x1, waiting for transfers between devices, on_device(): lax.psum_scatter(back_result[2].astype(jnp.bfloat16), 'context', scatter_...  74.7 us
    reduce_scatter x1, waiting for transfers between devices, on_device(): lax.psum_scatter(back_result[1].astype(jnp.bfloat16), 'context', scatter_...  67.5 us
    reduce_scatter x1, waiting for transfers between devices, on_device(): packed = lax.psum_scatter(packed, 'fsdp', scatter_dimension=0, tiled=True)  62.2 us
    all_gather x1, waiting for transfers between devices, on_device(): lax.all_gather(value_flat, 'context', axis=0, tiled=True)  42.2 us
    psum x1, waiting for transfers between devices, on_device(): lax.psum(jnp.dot(gate_up_grad, gelu_flat.T, preferred_element_type=jnp.fl...  41.8 us
    psum x1, waiting for transfers between devices, on_device(): residual = inputs + lax.psum(attn_part, 'tensor')  40.8 us
    all_gather x1, waiting for transfers between devices, on_device(): lax.all_gather(key_flat, 'context', axis=0, tiled=True)  33.9 us
  transfers between devices with their start and end apart: 11, of which 11 were waited for; matrix products, arithmetic and copies ran while one was open for 7% of the time, Pallas kernels for 0%

profile of v1, /device:TPU:0, one launch (start us, length us, event | category | flops | bytes accessed | tf_op | source)
XLA Modules:
  0.0 728.2 jit_solution(14247577715995963772)
XLA Ops:
  11.6 14.7 %all-reduce.2 = (bf16[768]{0:T(1024)(128)(2,1)S(1)}, bf16[768]{0:T(1024)(128)(2,1)S(1)}) all-reduce(bf16[768]{0:T(1024)(128)(2,1)S(1)} %dynamic-update-slice, bf16[768]{0:T(1024)(128)(2,1)S(1)} %dynamic-update-slice.1), channel_id=1, replica_groups=mesh['fsdp'=8,'tensor'=2,'context'=8] {'fsdp'}, use_global_device_ids=true, to_apply=%add | all-reduce | flops 1536 | bytes 6144
  30.6 6.5 all-gather.7.cloned.1.call-done
  37.1 2.6 copy.51
  45.6 13.2 %all_gather.36 = bf16[384,768]{0,1:T(8,128)(2,1)S(1)} all-gather(bf16[384,96]{0,1:T(8,128)(2,1)S(1)} %copy-done.46), channel_id=1, replica_groups=mesh['fsdp'=8,'tensor'=2,'context'=8] {'fsdp'}, dimensions={1}, use_global_device_ids=true | all-gather | bytes 663552 | tf_op jit(solution)/shard_map/all_gather | solution.py:125
  58.8 33.9 %all-gather.11.cloned.1.call-done = bf16[2048,384]{0,1:T(8,128)(2,1)} async-done(((bf16[256,384]{0,1:T(8,128)(2,1)}), bf16[2048,384]{0,1:T(8,128)(2,1)}) %all-gather.11.cloned.1.call-update) | async-done | bytes 1572880 | tf_op jit(solution)/shard_map/all_gather | solution.py:150
  92.7 3.9 select_reduce_fusion.1
  96.6 3.9 select_reduce_fusion
  101.1 42.2 %all-gather.9.cloned.1.call-done = bf16[2048,384]{0,1:T(8,128)(2,1)} async-done(((bf16[256,384]{0,1:T(8,128)(2,1)}), bf16[2048,384]{0,1:T(8,128)(2,1)}) %all-gather.9.cloned.1.call-update) | async-done | bytes 1572880 | tf_op jit(solution)/shard_map/all_gather | solution.py:151
  143.3 7.7 %fusion.13 = bf16[6,64,256]{2,1,0:T(8,128)(2,1)S(1)} fusion(bf16[2048,6,64]{0,2,1:T(8,128)(2,1)} %bitcast.186, f32[6,256,2048]{2,1,0:T(8,128)} %copy-done.7, f32[6,256]{1,0:T(8,128)S(1)} %log_add_fusion, pred[256,2048]{1,0:T(8,128)(4,1)S(1)} %broadcast_compare_fusion.1), kind=kOutput, calls=%fused_computation.37 | convolution fusion | flops 415334400 | bytes 14882816 | tf_op jit(solution)/shard_map/hqk,khd->qhd/dot_general | solution.py:168
  152.4 16.8 %all_gather.39 = bf16[576,768]{0,1:T(8,128)(2,1)} all-gather(bf16[576,96]{0,1:T(8,128)(2,1)S(1)} %copy-done.45), channel_id=1, replica_groups=mesh['fsdp'=8,'tensor'=2,'context'=8] {'fsdp'}, dimensions={1}, use_global_device_ids=true | all-gather | bytes 995328 | tf_op jit(solution)/shard_map/all_gather | solution.py:127
  170.0 2.7 copy.53
  172.7 40.8 %all-reduce.8.cloned.1.call-done = f32[256,768]{1,0:T(8,128)} async-done(((f32[256,768]{1,0:T(8,128)}), f32[256,768]{1,0:T(8,128)}) %all-reduce.8.cloned.1.call-update) | async-done | bytes 786448 | tf_op jit(solution)/shard_map/psum | solution.py:173
  219.8 41.8 %all-reduce.10.cloned.1.call-done = f32[256,768]{1,0:T(8,128)} async-done(((f32[256,768]{1,0:T(8,128)}), f32[256,768]{1,0:T(8,128)}) %all-reduce.10.cloned.1.call-update) | async-done | bytes 786448 | tf_op jit(solution)/shard_map/psum | solution.py:197
  266.4 2.1 broadcast.210
  270.5 40.4 %while.20 = (s32[]{:T(128)}, f32[256,6,64]{0,2,1:T(8,128)}, f32[2048,384]{0,1:T(8,128)}, f32[2048,384]{0,1:T(8,128)}, bf16[2048,384]{0,1:T(8,128)(2,1)}, /*index...) while((s32[]{:T(128)}, f32[256,6,64]{0,2,1:T(8,128)}, ...), condition=%wide.region_19.20_spmd.clone, body=%wide.region_17.19_spmd.clone.sunk | while | flops 1024107520 | bytes 131182336 | solution.py:85
  275.0 3.3 fusion.105
  278.4 2.6 fusion.106
  281.0 4.3 fusion.107
  295.2 3.3 fusion.105
  298.6 2.7 fusion.106
  301.2 4.3 fusion.107
  310.9 3.4 convert_element_type.160
  318.9 2.7 fusion.48
  321.6 67.5 %reduce-scatter.4.cloned.1.call-done = bf16[256,384]{0,1:T(8,128)(2,1)} async-done(((bf16[2048,384]{0,1:T(8,128)(2,1)}), bf16[256,384]{0,1:T(8,128)(2,1)}) %reduce-scatter.4.cloned.1.call-update) | async-done | bytes 196624 | tf_op jit(solution)/shard_map/reduce_scatter | solution.py:284
  391.1 74.7 %reduce-scatter.6.cloned.1.call-done = bf16[256,384]{0,1:T(8,128)(2,1)} async-done(((bf16[2048,384]{0,1:T(8,128)(2,1)}), bf16[256,384]{0,1:T(8,128)(2,1)}) %reduce-scatter.6.cloned.1.call-update) | async-done | bytes 196624 | tf_op jit(solution)/shard_map/reduce_scatter | solution.py:287
  469.1 3.0 convolution_bitcast_fusion
  473.7 2.6 fusion.45
  476.3 32.8 %all-reduce.12.cloned.1.call-done = (bf16[256,768]{1,0:T(8,128)(2,1)}, bf16[256,768]{1,0:T(8,128)(2,1)}) async-done(((bf16[256,768]{1,0:T(8,128)(2,1)}, bf16[256,768]{1,0:T(8,128)(2,1)}), (bf16[256,768]{1,0:T(8,128)(2,1)}, bf16[256,768]{1,0:T(8,128)(2,1)})) %all-reduce.12.cloned.1.call-update) | async-done | bytes 786448 | tf_op jit(solution)/shard_map/psum | solution.py:185
  510.7 13.5 %concatenate.21 = f32[768,3266]{1,0:T(8,128)} concatenate(f32[768,1]{1,0:T(8,128)S(1)} %broadcast_in_dim.141, f32[768,1]{1,0:T(8,128)S(1)} %broadcast_in_dim.142, f32[768,1152]{1,0:T(8,128)} %fusion.45, f32[768,1152]{1,0:T(8,128)} %fusion.48, f32[768,384]{1,0:T(8,128)} %fusion.38, f32[768,576]{1,0:T(8,128)} %convolution_bitcast_fusion), dimensions={1} | concatenate | bytes 20066304 | tf_op jit(solution)/shard_map/concatenate | solution.py:323
  524.3 62.2 %reduce-scatter.8.cloned.1.call-done = f32[96,3266]{1,0:T(8,128)} async-done(((f32[768,3266]{1,0:T(8,128)}), f32[96,3266]{1,0:T(8,128)}) %reduce-scatter.8.cloned.1.call-update) | async-done | bytes 1254160 | tf_op jit(solution)/shard_map/reduce_scatter | solution.py:324
  588.6 124.0 %all-gather.15.cloned.1.call-done = f32[768,3266]{1,0:T(8,128)} async-done(((f32[96,3266]{1,0:T(8,128)}), f32[768,3266]{1,0:T(8,128)}) %all-gather.15.cloned.1.call-update) | async-done | bytes 10033168 | tf_op jit(solution)/shard_map/all_gather | solution.py:112
  712.6 4.6 reduce_sum.174
  (265 shorter events, 68.5 us)
Async XLA Ops:
  7.2 32.6 %copy-start.10 = (bf16[256,768]{1,0:T(8,128)(2,1)S(1)}, bf16[256,768]{1,0:T(8,128)(2,1)}, u32[]{:S(2)}) copy-start(bf16[256,768]{1,0:T(8,128)(2,1)} %param.11) | copy-start | bytes 1179652
  7.2 29.9 %all-gather.7.cloned.1.call-start = ((), (), s32[]{:S(2)}) async-start(), calls=%async_computation.3 | async-start | bytes 1990656 | tf_op jit(solution)/shard_map/all_gather | solution.py:124
  7.9 84.8 %all-gather.11.cloned.1.call-start = ((), (), s32[]{:S(2)}) async-start(), calls=%async_computation.5 | async-start | bytes 1769472 | tf_op jit(solution)/shard_map/all_gather | solution.py:150
  30.3 10.2 %copy-start.50 = (f32[256]{0:T(256)}, f32[256]{0:T(256)S(1)}, u32[]{:S(2)}) copy-start(f32[256]{0:T(256)S(1)} %add_rsqrt_fusion.1) | copy-start | bytes 3076
  30.6 11.1 %copy-start.40 = (f32[256,32]{0,1:T(8,128)}, f32[256,32]{0,1:T(8,128)S(1)}, u32[]{:S(2)}) copy-start(f32[256,32]{0,1:T(8,128)S(1)} %get-tuple-element.409) | copy-start | bytes 98308
  30.6 11.1 %copy-start.41 = (f32[256,32]{0,1:T(8,128)}, f32[256,32]{0,1:T(8,128)S(1)}, u32[]{:S(2)}) copy-start(f32[256,32]{0,1:T(8,128)S(1)} %get-tuple-element.410) | copy-start | bytes 98308
  41.8 54.8 %copy-start.33 = (bf16[256,6,32]{0,2,1:T(8,128)(2,1)}, bf16[256,6,32]{0,2,1:T(8,128)(2,1)S(1)}, u32[]{:S(2)}) copy-start(bf16[256,6,32]{0,2,1:T(8,128)(2,1)S(1)} %get-tuple-element.401) | copy-start | bytes 294916
  41.8 54.8 %copy-start.35 = (bf16[256,6,32]{0,2,1:T(8,128)(2,1)}, bf16[256,6,32]{0,2,1:T(8,128)(2,1)S(1)}, u32[]{:S(2)}) copy-start(bf16[256,6,32]{0,2,1:T(8,128)(2,1)S(1)} %get-tuple-element.402) | copy-start | bytes 294916
  42.5 100.8 %all-gather.9.cloned.1.call-start = ((), (), s32[]{:S(2)}) async-start(), calls=%async_computation.4 | async-start | bytes 1769472 | tf_op jit(solution)/shard_map/all_gather | solution.py:151
  44.3 125.7 %all-gather.13.cloned.1.call-start = ((), (), s32[]{:S(2)}) async-start(), calls=%async_computation.7 | async-start | bytes 2211840 | tf_op jit(solution)/shard_map/all_gather | solution.py:126
  45.1 168.4 %all-reduce.8.cloned.1.call-start = ((), (), s32[]{:S(2)}) async-start(), calls=%async_computation.6 | async-start | bytes 1572864 | tf_op jit(solution)/shard_map/psum | solution.py:173
  58.8 92.1 %copy-start.19 = (bf16[384,768]{0,1:T(8,128)(2,1)}, bf16[384,768]{0,1:T(8,128)(2,1)S(1)}, u32[]{:S(2)}) copy-start(bf16[384,768]{0,1:T(8,128)(2,1)S(1)} %all_gather.36) | copy-start | bytes 1769476
  101.1 49.8 %copy-start.58 = (f32[6,256]{1,0:T(8,128)}, f32[6,256]{1,0:T(8,128)S(1)}, u32[]{:S(2)}) copy-start(f32[6,256]{1,0:T(8,128)S(1)} %log_add_fusion) | copy-start | bytes 18436
  143.3 9.1 %copy-start.45 = (bf16[576,96]{0,1:T(8,128)(2,1)S(1)}, bf16[576,96]{0,1:T(8,128)(2,1)}, u32[]{:S(2)}) copy-start(bf16[576,96]{0,1:T(8,128)(2,1)} %param.18) | copy-start | bytes 331780
  152.3 109.3 %all-reduce.10.cloned.1.call-start = ((), (), s32[]{:S(2)}) async-start(), calls=%async_computation.8 | async-start | bytes 1572864 | tf_op jit(solution)/shard_map/psum | solution.py:197
  172.7 44.1 %copy-start.31 = (bf16[256,768]{1,0:T(8,128)(2,1)S(1)}, bf16[256,768]{1,0:T(8,128)(2,1)}, u32[]{:S(2)}) copy-start(bf16[256,768]{1,0:T(8,128)(2,1)} %param.19) | copy-start | bytes 1179652
  214.9 48.9 %copy-start.8 = (f32[256,768]{1,0:T(8,128)}, f32[256,768]{1,0:T(8,128)S(1)}, u32[]{:S(2)}) copy-start(f32[256,768]{1,0:T(8,128)S(1)} %get-tuple-element.388) | copy-start | bytes 2359300
  217.5 46.2 %copy-start.42 = (bf16[256,1,576]{0,2,1:T(8,128)(2,1)}, bf16[256,1,576]{0,2,1:T(8,128)(2,1)S(1)}, u32[]{:S(2)}) copy-start(bf16[256,1,576]{0,2,1:T(8,128)(2,1)S(1)} %get-tuple-element.391) | copy-start | bytes 884740
  217.5 46.2 %copy-start.43 = (bf16[256,1,576]{0,2,1:T(8,128)(2,1)}, bf16[256,1,576]{0,2,1:T(8,128)(2,1)S(1)}, u32[]{:S(2)}) copy-start(bf16[256,1,576]{0,2,1:T(8,128)(2,1)S(1)} %get-tuple-element.392) | copy-start | bytes 884740
  217.5 44.1 %copy-start.48 = (f32[256]{0:T(256)S(1)}, f32[256]{0:T(256)}, u32[]{:S(2)}) copy-start(f32[256]{0:T(256)} %copy-done.47) | copy-start | bytes 3076
  217.5 44.1 %copy-start.53 = (f32[256]{0:T(256)S(1)}, f32[256]{0:T(256)}, u32[]{:S(2)}) copy-start(f32[256]{0:T(256)} %copy-done.52) | copy-start | bytes 3076
  217.8 45.9 %copy-start.32 = (bf16[256,768]{1,0:T(8,128)(2,1)S(1)}, bf16[256,768]{1,0:T(8,128)(2,1)}, u32[]{:S(2)}) copy-start(bf16[256,768]{1,0:T(8,128)(2,1)} %param.19) | copy-start | bytes 1179652
  219.6 45.6 %copy-start.20 = (bf16[384,768]{0,1:T(8,128)(2,1)S(1)}, bf16[384,768]{0,1:T(8,128)(2,1)}, u32[]{:S(2)}) copy-start(bf16[384,768]{0,1:T(8,128)(2,1)} %copy-done.19) | copy-start | bytes 1769476
  219.6 169.6 %reduce-scatter.4.cloned.1.call-start = ((), (), s32[]{:S(2)}) async-start(), calls=%async_computation.9 | async-start | bytes 1769472 | tf_op jit(solution)/shard_map/reduce_scatter | solution.py:284
  314.4 151.4 %reduce-scatter.6.cloned.1.call-start = ((), (), s32[]{:S(2)}) async-start(), calls=%async_computation.10 | async-start | bytes 1769472 | tf_op jit(solution)/shard_map/reduce_scatter | solution.py:287
  315.9 193.2 %all-reduce.12.cloned.1.call-start = ((), (), s32[]{:S(2)}) async-start(), calls=%async_computation.13 | async-start | bytes 1572864 | tf_op jit(solution)/shard_map/psum | solution.py:185
  318.9 71.2 %copy-start.14 = (f32[256,6,64]{0,2,1:T(8,128)S(1)}, f32[256,6,64]{0,2,1:T(8,128)}, u32[]{:S(2)}) copy-start(f32[256,6,64]{0,2,1:T(8,128)} %get-tuple-element.285) | copy-start | bytes 1179652
  318.9 148.7 %copy-start.13 = (bf16[768,3,384]{0,2,1:T(8,128)(2,1)S(1)}, bf16[768,3,384]{0,2,1:T(8,128)(2,1)}, u32[]{:S(2)}) copy-start(bf16[768,3,384]{0,2,1:T(8,128)(2,1)} %copy-done.12) | copy-start | bytes 5308420
  469.1 117.4 %reduce-scatter.8.cloned.1.call-start = ((), (), s32[]{:S(2)}) async-start(), calls=%async_computation.11 | async-start | bytes 11501568 | tf_op jit(solution)/shard_map/reduce_scatter | solution.py:324
  524.2 62.3 %copy-start.39 = (bf16[256,768]{1,0:T(8,128)(2,1)S(1)}, bf16[256,768]{1,0:T(8,128)(2,1)}, u32[]{:S(2)}) copy-start(bf16[256,768]{1,0:T(8,128)(2,1)} %get-tuple-element.385) | copy-start | bytes 1179652
  524.2 63.2 %copy-start.30 = (bf16[256,768]{1,0:T(8,128)(2,1)S(1)}, bf16[256,768]{1,0:T(8,128)(2,1)}, u32[]{:S(2)}) copy-start(bf16[256,768]{1,0:T(8,128)(2,1)} %get-tuple-element.386) | copy-start | bytes 1179652
  524.3 188.3 %all-gather.15.cloned.1.call-start = ((), (), s32[]{:S(2)}) async-start(), calls=%async_computation.12 | async-start | bytes 11501568 | tf_op jit(solution)/shard_map/all_gather | solution.py:112
  (57 other events, 174.0 us)
Sparse Core Ops, SparseCore 0:
  9.7 27.3 all-gather.6
  42.7 50.0 all-gather.10
  95.5 47.7 all-gather.8
  145.4 24.5 all-gather.12
  172.8 40.5 all-reduce.7
  219.7 41.8 all-reduce.9
  314.5 74.6 reduce-scatter.3
  393.3 72.4 reduce-scatter.5
  469.2 39.8 all-reduce.11
  524.4 62.0 reduce-scatter.7
  589.1 123.4 all-gather.14
